TPU v7x, 32 devices: a whole 2x2x4 slice. The times are simulated.
32 devices in a mesh: context: 4 (over x, core), tensor: 4 (over z), dp: 2 (over y).
Axes of the slice: x: 2, y: 2, z: 4, core: 2. Of those that a mesh axis runs over, the one named last changes fastest.
Arguments:
- queries: bfloat16 [1024, 64, 128], P(('dp', 'context'), 'tensor'), parts along dimension 0, may hold values from -160 to 160
- key_heads: bfloat16 [1024, 4, 128], P(('dp', 'context'), 'tensor'), parts along dimension 0, may hold values from -6 to 6
- value_heads: bfloat16 [1024, 4, 128], P(('dp', 'context'), 'tensor'), parts along dimension 0, may hold values from -6 to 6
- out_grad: bfloat16 [1024, 64, 128], P(('dp', 'context'), 'tensor'), parts along dimension 0, may hold values from -6 to 6
- layout: int32 [1024], P('dp'), parts along dimension 0, may hold values from 0 to 511, as said below
- documents: int32 [1024], P('dp'), parts along dimension 0, may hold values from 0 to 3, never falling along the last dimension, each value on 1 to 384 neighbouring positions
Outputs:
- output: bfloat16 [1024, 64, 128], P(('dp', 'context'), 'tensor'), parts along dimension 0
- query_grad: bfloat16 [1024, 64, 128], P(('dp', 'context'), 'tensor'), parts along dimension 0
- key_grad: float32 [1024, 512], P(('dp', 'context'), 'tensor'), parts along dimension 0
- value_grad: float32 [1024, 512], P(('dp', 'context'), 'tensor'), parts along dimension 0
There are 2 independent parts, one for each index of `dp`. A program takes and returns all parts, laid end to end along the dimension named above; each array names one. Nothing has to cross between parts.
Inputs may be any that keep to these rules, and one draw needn't show every extreme that they name: `layout`: a permutation of the tokens made of aligned runs of 64 consecutive tokens; every device's rows are two such runs, in an order drawn from the seed.
All inputs are finite; a program needn't handle non-finite values.
Results may differ from a plain program's by a relative error of at most 0.0064.
Values may be sent and summed in bfloat16 or wider, within the bound.
A program may use at most 128 MiB of HBM per device.

v0:
```python
import math

import jax
import jax.numpy as jnp
from jax import lax
from jax.sharding import PartitionSpec as P

THETA = 8000000.0


def rotary(source, places, direction):
    half_dim = source.shape[-1] // 2
    frequency = jnp.exp(
        -(2.0 * jnp.arange(half_dim, dtype=jnp.float32) / source.shape[-1]) * math.log(THETA)
    )
    angles = places.astype(jnp.float32)[:, None] * frequency[None, :]
    cosine = jnp.cos(angles)[:, None, :]
    sine_part = direction * jnp.sin(angles)[:, None, :]
    first_half = source[..., :half_dim]
    second = source[..., half_dim:]
    return jnp.concatenate(
        [first_half * cosine - second * sine_part, second * cosine + first_half * sine_part],
        axis=-1,
    )


def doc_positions(documents):
    length = documents.shape[0]
    indices = jnp.arange(length, dtype=jnp.int32)
    starts_here = jnp.concatenate([jnp.ones((1,), dtype=bool), documents[1:] != documents[:-1]])
    firsts = lax.cummax(jnp.where(starts_here, indices, jnp.zeros_like(indices)), axis=0)
    return indices - firsts


def body(queries, key_heads, value_heads, out_grad, layout, documents):
    local_rows, head_dev, head_dim = queries.shape
    scaling = 1.0 / math.sqrt(head_dim)
    first_row = lax.axis_index("context") * local_rows
    positions = doc_positions(documents)
    doc_rows = jnp.take(documents, layout)
    my_layout = lax.dynamic_slice_in_dim(layout, first_row, local_rows)
    my_docs = lax.dynamic_slice_in_dim(doc_rows, first_row, local_rows)
    my_places = jnp.take(positions, my_layout)
    value_mine = value_heads[:, 0]
    key_rot = rotary(key_heads.astype(jnp.float32), my_places, 1.0).astype(jnp.bfloat16)[:, 0]
    key_all, value_all = (
        lax.all_gather(key_rot, "context", axis=0, tiled=True),
        lax.all_gather(value_mine, "context", axis=0, tiled=True),
    )
    query_rot = rotary(queries.astype(jnp.float32), my_places, 1.0).astype(jnp.bfloat16)
    allowed = (my_docs[:, None] == doc_rows[None, :]) & (layout[None, :] <= my_layout[:, None])
    query_heads = jnp.transpose(query_rot, (1, 0, 2))
    grad_heads = jnp.transpose(out_grad, (1, 0, 2))

    def one_head(operands):
        query_one, grad_one = operands
        scores = jnp.dot(query_one, key_all.T, preferred_element_type=jnp.float32) * scaling
        scores = jnp.where(allowed, scores, -1e30)
        largest = jnp.max(scores, axis=1, keepdims=True)
        weights = jnp.exp(scores - largest)
        attention = weights / jnp.sum(weights, axis=1, keepdims=True)
        attention_b = attention.astype(jnp.bfloat16)
        result = jnp.dot(attention_b, value_all, preferred_element_type=jnp.float32).astype(
            jnp.bfloat16
        )
        dprobs = jnp.dot(grad_one, value_all.T, preferred_element_type=jnp.float32)
        row_delta = jnp.sum(
            grad_one.astype(jnp.float32) * result.astype(jnp.float32), axis=1, keepdims=True
        )
        dscores = (attention * (dprobs - row_delta) * scaling).astype(jnp.bfloat16)
        query_prod = jnp.dot(dscores, key_all, preferred_element_type=jnp.float32)
        return (result, query_prod, attention_b, dscores)

    results, query_prods, attn_all, dscore_all = lax.map(one_head, (query_heads, grad_heads))
    output = jnp.transpose(results, (1, 0, 2))
    query_grad = rotary(jnp.transpose(query_prods, (1, 0, 2)), my_places, -1.0).astype(jnp.bfloat16)
    combined = lax.psum_scatter(
        jnp.concatenate(
            [
                jnp.einsum(
                    "hqk,hqd->kd", dscore_all, query_heads, preferred_element_type=jnp.float32
                ),
                jnp.einsum("hqk,hqd->kd", attn_all, grad_heads, preferred_element_type=jnp.float32),
            ],
            axis=1,
        ),
        "context",
        scatter_dimension=0,
        tiled=True,
    )
    key_sum = combined[:, :head_dim]
    value_grad = combined[:, head_dim:]
    key_grad = rotary(key_sum[:, None, :], my_places, -1.0)[:, 0]
    return (output, query_grad, key_grad, value_grad)


def solution(mesh):
    return jax.shard_map(
        body,
        mesh=mesh,
        in_specs=(
            P(("dp", "context"), "tensor", None),
            P(("dp", "context"), "tensor", None),
            P(("dp", "context"), "tensor", None),
            P(("dp", "context"), "tensor", None),
            P("dp"),
            P("dp"),
        ),
        out_specs=(
            P(("dp", "context"), "tensor", None),
            P(("dp", "context"), "tensor", None),
            P(("dp", "context"), "tensor"),
            P(("dp", "context"), "tensor"),
        ),
        check_vma=False,
    )
```

profile of v0, /device:TPU:0, one launch (start us, length us, event | category | flops | bytes accessed | tf_op | source)
XLA Modules:
  0.0 132.0 jit_solution(769509619941778496)
XLA Ops:
  10.3 3.6 %gather_fusion.1 = s32[512]{0:T(512)S(1)} fusion(s32[512]{0:T(512)} %param.13, s32[1024]{0:T(1024)S(1)} %pad_clamp_fusion), kind=kCustom, calls=%fused_computation.1 | custom fusion | bytes 6144 | tf_op jit(solution)/shard_map/jit(_take)/gather | solution.py:40
  14.1 1.3 gather_fusion
  15.9 6.5 %all_gather.6 = bf16[512,128]{0,1:T(8,128)(2,1)S(1)} all-gather(bf16[128,128]{0,1:T(8,128)(2,1)S(1)} %pad_maximum_fusion.2), channel_id=1, replica_groups=mesh['context'=4,'tensor'=4,'dp'=2] {'context'}, dimensions={0}, use_global_device_ids=true | all-gather | bytes 163840 | tf_op jit(solution)/shard_map/all_gather | solution.py:47
  22.5 5.6 %all-gather = bf16[512,1,128]{2,0,1:T(8,128)(2,1)S(1)} all-gather(bf16[128,1,128]{2,0,1:T(8,128)(2,1)S(1)} %copy-done.4), channel_id=2, replica_groups=mesh['context'=4,'tensor'=4,'dp'=2] {'context'}, dimensions={0}, use_global_device_ids=true | all-gather | bytes 163840 | tf_op jit(solution)/shard_map/all_gather | solution.py:48
  28.6 1.5 %copy.20 = bf16[128,16,128]{0,2,1:T(8,128)(2,1)S(1)} copy(bf16[128,16,128]{2,1,0:T(8,128)(2,1)} %param.8) | data formatting | bytes 1048576 | tf_op args[0]
  31.1 65.3 %while.17 = (s32[]{:T(128)}, bf16[16,128,128]{1,2,0:T(8,128)(2,1)}, f32[16,128,128]{1,2,0:T(8,128)}, bf16[16,128,512]{2,1,0:T(8,128)(2,1)}, bf16[16,128,512]{2,1...) while((s32[]{:T(128)}, bf16[16,128,128]{1,2,0:T(8,128)(2,1)}, ...), condition=%wide.region_6.7_spmd.clone, body=%wide.region_2.6_spmd.clone.sunk | while | flops 68501120 | bytes 2633377 | solution.py:74
  31.1 1.1 fusion.58
  35.2 1.1 fusion.58
  39.3 1.1 fusion.58
  43.4 1.1 fusion.58
  47.4 1.1 fusion.58
  51.5 1.1 fusion.58
  55.6 1.1 fusion.58
  63.8 1.1 fusion.58
  71.9 1.1 fusion.58
  76.0 1.1 fusion.58
  80.1 1.1 fusion.58
  84.2 1.1 fusion.58
  88.3 1.1 fusion.58
  92.4 1.1 fusion.58
  96.9 1.1 copy-done
  99.6 1.2 copy.27
  100.7 1.2 copy.25
  101.9 20.7 %reduce-scatter.2.cloned.1.call-done = f32[128,256]{0,1:T(8,128)} async-done(((f32[512,256]{0,1:T(8,128)}), f32[128,256]{0,1:T(8,128)}) %reduce-scatter.2.cloned.1.call-update) | async-done | bytes 131088 | tf_op jit(solution)/shard_map/reduce_scatter | solution.py:77
  (152 shorter events, 60.1 us)
Async XLA Ops:
  7.2 6.7 %copy-start.6 = (s32[512]{0:T(512)S(1)}, s32[512]{0:T(512)}, u32[]{:S(2)}) copy-start(s32[512]{0:T(512)} %param.12) | copy-start | bytes 6148
  7.2 6.8 %copy-start.5 = (bf16[128,1,128]{2,0,1:T(8,128)(2,1)S(1)}, bf16[128,1,128]{2,0,1:T(8,128)(2,1)}, u32[]{:S(2)}) copy-start(bf16[128,1,128]{2,0,1:T(8,128)(2,1)} %param.9) | copy-start | bytes 98308
  7.2 15.3 %copy-start.4 = (bf16[128,1,128]{2,0,1:T(8,128)(2,1)S(1)}, bf16[128,1,128]{2,0,1:T(8,128)(2,1)}, u32[]{:S(2)}) copy-start(bf16[128,1,128]{2,0,1:T(8,128)(2,1)} %param.10) | copy-start | bytes 98308
  7.2 20.9 %copy-start.2 = (bf16[128,16,128]{2,1,0:T(8,128)(2,1)S(1)}, bf16[128,16,128]{2,1,0:T(8,128)(2,1)}, u32[]{:S(2)}) copy-start(bf16[128,16,128]{2,1,0:T(8,128)(2,1)} %param.11) | copy-start | bytes 1572868
  7.2 115.4 %reduce-scatter.2.cloned.1.call-start = ((), (), s32[]{:S(2)}) async-start(), calls=%async_computation.1 | async-start | bytes 655360 | tf_op jit(solution)/shard_map/reduce_scatter | solution.py:77
  96.4 1.6 %copy-start = (bf16[16,128,512]{2,1,0:T(8,128)(2,1)S(1)}, bf16[16,128,512]{2,1,0:T(8,128)(2,1)}, u32[]{:S(2)}) copy-start(bf16[16,128,512]{2,1,0:T(8,128)(2,1)} %get-tuple-element.62) | copy-start | bytes 6291460
  98.0 1.3 copy-start.1
  99.3 1.4 %copy-start.3 = (bf16[16,128,128]{1,2,0:T(8,128)(2,1)S(1)}, bf16[16,128,128]{1,2,0:T(8,128)(2,1)}, u32[]{:S(2)}) copy-start(bf16[16,128,128]{1,2,0:T(8,128)(2,1)} %get-tuple-element.59) | copy-start | bytes 1572868
Sparse Core Ops, SparseCore 0:
  99.5 23.1 reduce-scatter.1
where the time goes:
time: 133 us; the launch traced here: 132 us
  matrix products  49.8 us (37%)
  other arithmetic  21.8 us (16%)
  waiting for transfers between devices  20.7 us (16%)
  between operations  14.3 us (11%)
  local copies, waits for them, and re-layouts  13.2 us (10%)
  blocking collectives  12.1 us (9%)
    reduce_scatter x1, waiting for transfers between devices, body(): lax.psum_scatter(jnp.concatenate([jnp.einsum('hqk,hqd->kd', dscore_all, q...  20.7 us
    dot_general x16, matrix products, one_head(): jnp.dot(query_one, key_all.T, preferred_element_type=jnp.float32) * scaling  17 us
    dot_general x16, matrix products, one_head(): jnp.dot(attention_b, value_all, preferred_element_type=jnp.float32)  14.5 us
    dot_general x16, matrix products, one_head(): query_prod = jnp.dot(dscores, key_all, preferred_element_type=jnp.float32)  13.9 us
    dynamic_update_slice x16, other arithmetic, body(): lax.map(one_head, (query_heads, grad_heads))  12.5 us
    all_gather x1, blocking collectives, body(): lax.all_gather(key_rot, 'context', axis=0, tiled=True)  6.51 us
    unnamed x21, local copies, waits for them, and re-layouts  5.97 us
    all_gather x1, blocking collectives, body(): lax.all_gather(value_mine, 'context', axis=0, tiled=True)  5.59 us
  transfers between devices with their start and end apart: 1, of which 1 were waited for; matrix products, arithmetic and copies ran while one was open for 2% of the time, Pallas kernels for 0%

commit v1 on v0

v1 whole, which is shorter than its diff:
```python
import functools
import math

import jax
import jax.numpy as jnp
from jax import lax
from jax.experimental import pallas as pl
from jax.experimental.pallas import tpu as pltpu
from jax.sharding import PartitionSpec as P

THETA = 8000000.0
RUN = 64
MASKED = -1e30
MESH = pl.DeviceIdType.MESH
F32 = jnp.float32
BF16 = jnp.bfloat16


def dot(lhs, rhs, rhs_dim=0):
    return lax.dot_general(lhs, rhs, (((1,), (rhs_dim,)), ((), ())), preferred_element_type=F32)


def loop(count, step):
    if count <= 8:
        for index in range(count):
            step(index)
    else:
        lax.fori_loop(0, count, lambda index, _: (step(index), None)[1], None)


def rotate(x, cosine, sine):
    return x * cosine + pltpu.roll(x, x.shape[-1] // 2, 1) * sine


def kernel(n, heads, chunk, layout_s, layout_v, docs_v, q_hbm, k_ref, v_hbm, g_hbm,
           o_hbm, dq_hbm, dk_out, dv_out,
           q_in, g_in, qe, kall, vall, k_t, v_t, bias_t, cos_ref, sin_ref, probs, o_buf, dq_buf,
           send_buf, recv_buf, own_dv, local_sem, send_sem, recv_sem):
    me = lax.axis_index("context")
    rows, hd = k_ref.shape
    seq = rows * n
    flat = rows * heads
    tokens = chunk // heads
    scale = 1.0 / math.sqrt(hd)

    barrier = pltpu.get_barrier_semaphore()
    for k in range(1, n):
        pl.semaphore_signal(barrier, inc=1, device_id={"context": lax.rem(me + k, n)}, device_id_type=MESH)

    def block(index):
        return pl.ds(pl.multiple_of(index * rows, rows), rows)

    mine = block(me)
    q_copy = pltpu.make_async_copy(q_hbm, q_in, local_sem.at[0])
    g_copy = pltpu.make_async_copy(g_hbm, g_in, local_sem.at[1])
    v_copy = pltpu.make_async_copy(v_hbm, vall.at[mine], local_sem.at[2])
    v_copy.start()
    q_copy.start()
    g_copy.start()

    first = layout_s[me * rows].astype(F32)
    second = layout_s[me * rows + RUN].astype(F32)
    row_at = lax.broadcasted_iota(jnp.int32, (rows, hd), 0)
    token = jnp.where(row_at < RUN, row_at.astype(F32) + first, (row_at - RUN).astype(F32) + second)
    token = token[:, :1]
    docs = jnp.broadcast_to(docs_v[...], (8, seq))
    lane_at = lax.broadcasted_iota(jnp.int32, (8, seq), 1)
    starts = jnp.where(docs != pltpu.roll(docs, 1, 1), lane_at, 0).astype(F32)[:1]
    start = jnp.max(jnp.where(starts <= token, starts, 0.0), axis=1, keepdims=True)
    half = hd // 2
    lane = lax.broadcasted_iota(jnp.int32, (1, hd), 1)
    freq = jnp.exp(-(2.0 * lax.rem(lane, half).astype(F32) / hd) * math.log(THETA))
    angles = (token - start) * freq
    cosine = jnp.cos(angles)
    sine = jnp.where(lane < half, -1.0, 1.0) * jnp.sin(angles)
    cos_ref[...] = cosine
    sin_ref[...] = sine
    kall[mine] = rotate(k_ref[...].astype(F32), cosine, sine).astype(BF16)

    pl.semaphore_wait(barrier, n - 1)

    def transfer(kind, k, source, target):
        return pltpu.make_async_remote_copy(
            src_ref=source, dst_ref=target,
            send_sem=send_sem.at[kind, k], recv_sem=recv_sem.at[kind, k],
            device_id={"context": lax.rem(me + k + 1, n)}, device_id_type=MESH)

    def order(k):
        return (k + 1) % (n - 1) if n <= 8 else k

    def k_send(k):
        return transfer(0, k, kall.at[mine], kall.at[mine])

    def v_send(k):
        return transfer(1, k, vall.at[mine], vall.at[mine])

    def g_send(kind, k):
        return transfer(2 + kind, k, send_buf.at[kind, k], recv_buf.at[kind, k])

    loop(n - 1, lambda k: k_send(k).start())
    v_copy.wait()
    loop(n - 1, lambda k: v_send(k).start())

    keys = layout_v[...].astype(F32)
    bias = jnp.where((keys >= start) & (keys <= token), 0.0, MASKED)
    bias_t[...] = bias.T.astype(BF16)
    q_copy.wait()

    def spread(ref, at):
        part = ref[pl.ds(pl.multiple_of(at * tokens, tokens), tokens), :]
        return jnp.broadcast_to(part[:, None, :], (tokens, heads, hd)).reshape(chunk, hd)

    def span(at):
        return pl.ds(pl.multiple_of(at * chunk, chunk), chunk)

    def make_q(at, _):
        here = span(at)
        qe[here, :hd] = rotate(q_in[here, :].astype(F32), spread(cos_ref, at), spread(sin_ref, at)).astype(BF16)
        row = lax.broadcasted_iota(jnp.int32, (chunk, hd), 0) // heads + at * tokens
        col = lax.broadcasted_iota(jnp.int32, (chunk, hd), 1)
        qe[here, hd:] = (row == col).astype(F32).astype(BF16)

    steps = flat // chunk
    lax.fori_loop(0, steps, make_q, None)
    g_copy.wait()
    loop(n - 1, lambda k: k_send(k).wait_recv())
    k_t[...] = kall[...].astype(F32).T.astype(BF16)

    def make_probs(at, _):
        here = span(at)
        keys_bias = jnp.concatenate([kall[...], bias_t[...]], axis=1)
        scores = dot(keys_bias, qe[here, :], 1)
        largest = jnp.max(scores, axis=0, keepdims=True)
        weights = jnp.exp2((scores - largest) * (scale * math.log2(math.e)))
        total = jnp.sum(weights, axis=0, keepdims=True)
        probs[:, here] = (weights * (1.0 / total)).astype(BF16)

    lax.fori_loop(0, steps, make_probs, None)

    def v_grads(k):
        peer = lax.rem(me + k + 1, n)
        send_buf[0, k] = dot(probs[block(peer), :], g_in[...]).astype(BF16)
        g_send(0, k).start()

    loop(n - 1, v_grads)
    own_dv[...] = dot(probs[mine, :], g_in[...])
    loop(n - 1, lambda k: v_send(k).wait_recv())
    v_t[...] = vall[...].astype(F32).T.astype(BF16)

    def make_ds(at, _):
        here = span(at)
        p_b = probs[:, here]
        o_buf[here, :] = dot(v_t[...], p_b).T.astype(BF16)
        dprobs = dot(vall[...], g_in[here, :], 1)
        p = p_b.astype(F32)
        delta = jnp.sum(p * dprobs, axis=0, keepdims=True)
        probs[:, here] = (p * (dprobs - delta) * scale).astype(BF16)

    lax.fori_loop(0, steps, make_ds, None)
    o_copy = pltpu.make_async_copy(o_buf, o_hbm, local_sem.at[3])
    o_copy.start()

    def k_grads(k):
        peer = lax.rem(me + k + 1, n)
        send_buf[1, k] = dot(probs[block(peer), :], qe[:, :hd]).astype(BF16)
        g_send(1, k).start()

    loop(n - 1, k_grads)
    own_dk = dot(probs[mine, :], qe[:, :hd])

    def make_dq(at, _):
        here = span(at)
        grad = dot(k_t[...], probs[:, here]).T
        dq_buf[here, :] = rotate(grad, spread(cos_ref, at), -spread(sin_ref, at)).astype(BF16)

    lax.fori_loop(0, steps, make_dq, None)
    dq_copy = pltpu.make_async_copy(dq_buf, dq_hbm, local_sem.at[4])
    dq_copy.start()

    def collect(kind, own):
        loop(n - 1, lambda k: g_send(kind, k).wait_recv())
        return own + jnp.sum(recv_buf[kind].astype(F32), axis=0)

    dv_out[...] = collect(0, own_dv[...])
    dk_out[...] = rotate(collect(1, own_dk), cos_ref[...], -sin_ref[...])

    def finish(k):
        k_send(k).wait_send()
        v_send(k).wait_send()
        g_send(0, k).wait_send()
        g_send(1, k).wait_send()

    loop(n - 1, finish)
    o_copy.wait()
    dq_copy.wait()


def body(n, queries, key_heads, value_heads, out_grad, layout, documents):
    rows, heads, hd = queries.shape
    seq = layout.shape[0]
    flat = rows * heads
    chunk = 256 if seq <= 1024 else 128
    any_spec = pl.BlockSpec(memory_space=pl.ANY)
    vmem_spec = pl.BlockSpec(memory_space=pltpu.VMEM)
    out, dq, dk, dv = pl.pallas_call(
        functools.partial(kernel, n, heads, chunk),
        out_shape=(
            jax.ShapeDtypeStruct((flat, hd), BF16),
            jax.ShapeDtypeStruct((flat, hd), BF16),
            jax.ShapeDtypeStruct((rows, hd), F32),
            jax.ShapeDtypeStruct((rows, hd), F32),
        ),
        in_specs=[pl.BlockSpec(memory_space=pltpu.SMEM), vmem_spec, vmem_spec,
                  any_spec, vmem_spec, any_spec, any_spec],
        out_specs=(any_spec, any_spec, vmem_spec, vmem_spec),
        scratch_shapes=[
            pltpu.VMEM((flat, hd), BF16),
            pltpu.VMEM((flat, hd), BF16),
            pltpu.VMEM((flat, 2 * hd), BF16),
            pltpu.VMEM((seq, hd), BF16),
            pltpu.VMEM((seq, hd), BF16),
            pltpu.VMEM((hd, seq), BF16),
            pltpu.VMEM((hd, seq), BF16),
            pltpu.VMEM((seq, rows), BF16),
            pltpu.VMEM((rows, hd), F32),
            pltpu.VMEM((rows, hd), F32),
            pltpu.VMEM((seq, flat), BF16),
            pltpu.VMEM((flat, hd), BF16),
            pltpu.VMEM((flat, hd), BF16),
            pltpu.VMEM((2, n - 1, rows, hd), BF16),
            pltpu.VMEM((2, n - 1, rows, hd), BF16),
            pltpu.VMEM((rows, hd), F32),
            pltpu.SemaphoreType.DMA((5,)),
            pltpu.SemaphoreType.DMA((4, n - 1)),
            pltpu.SemaphoreType.DMA((4, n - 1)),
        ],
        compiler_params=pltpu.CompilerParams(
            collective_id=0, has_side_effects=True, vmem_limit_bytes=52 * 1024 * 1024),
    )(
        layout, layout.reshape(1, seq), documents.reshape(1, seq),
        queries.reshape(flat, hd), key_heads.reshape(rows, hd), value_heads.reshape(rows, hd),
        out_grad.reshape(flat, hd),
    )
    return (out.reshape(rows, heads, hd), dq.reshape(rows, heads, hd), dk, dv)


def solution(mesh):
    return jax.shard_map(
        functools.partial(body, mesh.shape["context"]),
        mesh=mesh,
        in_specs=(
            P(("dp", "context"), "tensor", None),
            P(("dp", "context"), "tensor", None),
            P(("dp", "context"), "tensor", None),
            P(("dp", "context"), "tensor", None),
            P("dp"),
            P("dp"),
        ),
        out_specs=(
            P(("dp", "context"), "tensor", None),
            P(("dp", "context"), "tensor", None),
            P(("dp", "context"), "tensor"),
            P(("dp", "context"), "tensor"),
        ),
        check_vma=False,
    )
```

time: 133 us -> 26.6 us (0.20)
  matrix products: 49.8 us -> 0 us
  other arithmetic: 21.8 us -> 0 us
  waiting for transfers between devices: 20.7 us -> 0 us
  Pallas kernels: 0 us -> 19.5 us
  between operations: 14.3 us -> 0.66 us
  blocking collectives: 12.1 us -> 0 us
  local copies, waits for them, and re-layouts: 13.2 us -> 6.08 us
    dot_general x66 -> x0, matrix products: 49.8 us -> none  [the longest x16 17 us: one_head(): jnp.dot(query_one, key_all.T, preferred_element_type=jnp.float32) * scaling]
    reduce_scatter x1 -> x0, waiting for transfers between devices: 20.7 us -> none  [body(): lax.psum_scatter(jnp.concatenate([jnp.einsum('hqk,hqd->kd', dscore_all, q...]
    pallas_call x0 -> x1, Pallas kernels: none -> 19.5 us  [body(): pl.pallas_call(functools.partial(kernel, n, heads, chunk), out_shape=(jax...]
    dynamic_update_slice x16 -> x0, other arithmetic: 12.5 us -> none  [body(): lax.map(one_head, (query_heads, grad_heads))]
    all_gather x2 -> x0, blocking collectives: 12.1 us -> none  [the longest x1 6.51 us: body(): lax.all_gather(key_rot, 'context', axis=0, tiled=True)]
    gather x2 -> x0, local copies, waits for them, and re-layouts: 4.89 us -> none  [the longest x1 3.62 us: body(): doc_rows = jnp.take(documents, layout)]
    reduce_sum x32 -> x0, other arithmetic: 3.74 us -> none  [the longest x16 3.14 us: one_head(): attention = weights / jnp.sum(weights, axis=1, keepdims=True)]
    select_n x4 -> x0, other arithmetic: 1.52 us -> none  [the longest x1 0.76 us: body(): my_places = jnp.take(positions, my_layout)]
  transfers between devices with their start and end apart: 1 -> 0, of which waited for: 1 -> 0; matrix products, arithmetic and copies ran while one was open for 2% -> 0% of each run, Pallas kernels for 0% -> 0%
where the time goes in v1:
time: 26.6 us; the launch traced here: 26.2 us
  Pallas kernels  19.5 us (73%)
  local copies, waits for them, and re-layouts  6.08 us (23%)
  between operations  0.66 us (2%)
    pallas_call x1, Pallas kernels, body(): pl.pallas_call(functools.partial(kernel, n, heads, chunk), out_shape=(jax...  19.5 us
    unnamed x14, local copies, waits for them, and re-layouts  6.08 us

profile of v1, /device:TPU:0, one launch (start us, length us, event | category | flops | bytes accessed | tf_op | source)
XLA Modules:
  0.0 26.2 jit_solution(11692148690142381009)
XLA Ops:
  0.6 0.0 copy-start.4
  0.6 0.0 copy-start.3
  0.7 0.7 %copy-done.4 = s32[512]{0:T(512)S(1)} copy-done((s32[512]{0:T(512)S(1)}, s32[512]{0:T(512)}, u32[]{:S(2)}) %copy-start.4) | copy-done | bytes 2072
  1.3 0.0 copy-done.3
  1.3 0.0 copy-start
  1.3 1.0 %copy-done = bf16[128,16,128]{2,1,0:T(8,128)(2,1)S(1)} copy-done((bf16[128,16,128]{2,1,0:T(8,128)(2,1)S(1)}, bf16[128,16,128]{2,1,0:T(8,128)(2,1)}, u32[]{:S(2)}) %copy-start) | copy-done | bytes 524312
  2.4 0.0 copy-start.1
  2.4 0.8 %copy-done.1 = bf16[128,1,128]{2,0,1:T(8,128)(2,1)S(1)} copy-done((bf16[128,1,128]{2,0,1:T(8,128)(2,1)S(1)}, bf16[128,1,128]{2,0,1:T(8,128)(2,1)}, u32[]{:S(2)}) %copy-start.1) | copy-done | bytes 32792
  3.1 0.0 copy-start.2
  3.1 0.8 %copy-done.2 = bf16[128,1,128]{2,0,1:T(8,128)(2,1)S(1)} copy-done((bf16[128,1,128]{2,0,1:T(8,128)(2,1)S(1)}, bf16[128,1,128]{2,0,1:T(8,128)(2,1)}, u32[]{:S(2)}) %copy-start.2) | copy-done | bytes 32792
  3.9 19.5 %shard_map.93 = (bf16[2048,128]{1,0:T(8,128)(2,1)S(1)}, bf16[2048,128]{1,0:T(8,128)(2,1)S(1)}, f32[128,128]{1,0:T(8,128)S(1)}, f32[128,128]{1,0:T(8,128)S(1)}) custom-call(s32[512]{0:T(512)S(1)} %copy-done.3, s32[1,512]{1,0:T(1,128)S(1)} %bitcast.13, s32[1,512]{1,0:T(1,128)S(1)} %bitcast.14, bf16[2048,128]{1,0:T(8,128)(2,1)S(1)} %bitcast.8, ...), custom_call_target="tpu_custom_call" | custom-call | tf_op jit(solution)/shard_map/pallas_call | solution.py:205
  23.4 0.8 %copy.14 = bf16[128,16,128]{2,1,0:T(8,128)(2,1)} copy(bf16[128,16,128]{2,1,0:T(8,128)(2,1)S(1)} %bitcast.10) | data formatting | bytes 1048576
  24.2 0.8 %copy.15 = bf16[128,16,128]{2,1,0:T(8,128)(2,1)} copy(bf16[128,16,128]{2,1,0:T(8,128)(2,1)S(1)} %bitcast.9) | data formatting | bytes 1048576
  25.0 0.6 %copy.16 = f32[128,128]{1,0:T(8,128)} copy(f32[128,128]{1,0:T(8,128)S(1)} %get-tuple-element.18) | data formatting | bytes 131072
  25.6 0.6 %copy.17 = f32[128,128]{1,0:T(8,128)} copy(f32[128,128]{1,0:T(8,128)S(1)} %get-tuple-element.19) | data formatting | bytes 131072
Async XLA Ops:
  0.6 0.7 %copy-start.4 = (s32[512]{0:T(512)S(1)}, s32[512]{0:T(512)}, u32[]{:S(2)}) copy-start(s32[512]{0:T(512)} %param.11) | copy-start | bytes 6148
  0.6 0.7 %copy-start.3 = (s32[512]{0:T(512)S(1)}, s32[512]{0:T(512)}, u32[]{:S(2)}) copy-start(s32[512]{0:T(512)} %layout_s.1) | copy-start | bytes 6148
  1.3 1.0 %copy-start = (bf16[128,16,128]{2,1,0:T(8,128)(2,1)S(1)}, bf16[128,16,128]{2,1,0:T(8,128)(2,1)}, u32[]{:S(2)}) copy-start(bf16[128,16,128]{2,1,0:T(8,128)(2,1)} %param.6) | copy-start | bytes 1572868
  2.4 0.8 %copy-start.1 = (bf16[128,1,128]{2,0,1:T(8,128)(2,1)S(1)}, bf16[128,1,128]{2,0,1:T(8,128)(2,1)}, u32[]{:S(2)}) copy-start(bf16[128,1,128]{2,0,1:T(8,128)(2,1)} %param.7) | copy-start | bytes 98308
  3.1 0.8 %copy-start.2 = (bf16[128,1,128]{2,0,1:T(8,128)(2,1)S(1)}, bf16[128,1,128]{2,0,1:T(8,128)(2,1)}, u32[]{:S(2)}) copy-start(bf16[128,1,128]{2,0,1:T(8,128)(2,1)} %param.8) | copy-start | bytes 98308

commit v2 on v1

v2 whole, which is shorter than its diff:
```python
import functools
import math

import jax
import jax.numpy as jnp
from jax import lax
from jax.experimental import pallas as pl
from jax.experimental.pallas import tpu as pltpu
from jax.sharding import PartitionSpec as P

THETA = 8000000.0
RUN = 64
MASKED = -1e30
MESH = pl.DeviceIdType.MESH
F32 = jnp.float32
BF16 = jnp.bfloat16


def dot(lhs, rhs, rhs_dim=0):
    return lax.dot_general(lhs, rhs, (((1,), (rhs_dim,)), ((), ())), preferred_element_type=F32)


def loop(count, step):
    if count <= 8:
        for index in range(count):
            step(index)
    else:
        lax.fori_loop(0, count, lambda index, _: (step(index), None)[1], None)


def span(at, size):
    start = at * size
    return pl.ds(start if isinstance(at, int) else pl.multiple_of(start, size), size)


def rotate(x, cosine, sine):
    return x * cosine + pltpu.roll(x, x.shape[-1] // 2, 1) * sine


def spread(ref, at, chunk, heads):
    part = ref[span(at, chunk // heads), :]
    return jnp.broadcast_to(part[:, None, :], (chunk // heads, heads, part.shape[-1])).reshape(chunk, -1)


def main_kernel(n, heads, chunk, layout_h, layout_row_h, docs_h, q_h, k_h, v_h, g_h,
                o_ref, probs, k_t, cos_ref, sin_ref, dk_ref, dv_ref,
                layout_s, layout_v, docs_v, k_in, q_in, g_in, qe, kall, vall, v_t, p_t, bias_t,
                send_buf, recv_buf, own_dv, local_sem, send_sem, recv_sem):
    me = lax.axis_index("context")
    rows, hd = k_in.shape
    seq = rows * n
    flat = rows * heads
    tokens = chunk // heads
    steps = flat // chunk
    scale = 1.0 / math.sqrt(hd)

    barrier = pltpu.get_barrier_semaphore()
    for k in range(1, n):
        pl.semaphore_signal(barrier, inc=1, device_id={"context": lax.rem(me + k, n)}, device_id_type=MESH)

    mine = span(me, rows)
    layout_copy = pltpu.make_async_copy(layout_h, layout_s, local_sem.at[0])
    docs_copy = pltpu.make_async_copy(docs_h, docs_v, local_sem.at[1])
    k_copy = pltpu.make_async_copy(k_h, k_in, local_sem.at[2])
    row_copy = pltpu.make_async_copy(layout_row_h, layout_v, local_sem.at[3])
    v_copy = pltpu.make_async_copy(v_h, vall.at[mine], local_sem.at[4])
    q_copy = pltpu.make_async_copy(q_h, q_in, local_sem.at[5])
    g_copy = pltpu.make_async_copy(g_h, g_in, local_sem.at[6])
    for copy in (layout_copy, docs_copy, k_copy, v_copy, row_copy, q_copy, g_copy):
        copy.start()

    half = hd // 2
    lane = lax.broadcasted_iota(jnp.int32, (1, hd), 1)
    freq = jnp.exp(-(2.0 * lax.rem(lane, half).astype(F32) / hd) * math.log(THETA))
    row_at = lax.broadcasted_iota(jnp.int32, (rows, hd), 0)
    layout_copy.wait()
    first = layout_s[me * rows].astype(F32)
    second = layout_s[me * rows + RUN].astype(F32)
    token = jnp.where(row_at < RUN, row_at.astype(F32) + first, (row_at - RUN).astype(F32) + second)
    token = token[:, :1]
    docs_copy.wait()
    docs = jnp.broadcast_to(docs_v[...], (8, seq))
    lane_at = lax.broadcasted_iota(jnp.int32, (8, seq), 1)
    starts = jnp.where(docs != pltpu.roll(docs, 1, 1), lane_at, 0).astype(F32)[:1]
    start = jnp.max(jnp.where(starts <= token, starts, 0.0), axis=1, keepdims=True)
    angles = (token - start) * freq
    cosine = jnp.cos(angles)
    sine = jnp.where(lane < half, -1.0, 1.0) * jnp.sin(angles)
    cos_ref[...] = cosine
    sin_ref[...] = sine
    k_copy.wait()
    kall[mine] = rotate(k_in[...].astype(F32), cosine, sine).astype(BF16)
    v_copy.wait()

    pl.semaphore_wait(barrier, n - 1)

    def transfer(kind, k, source, target):
        return pltpu.make_async_remote_copy(
            src_ref=source, dst_ref=target,
            send_sem=send_sem.at[kind, k], recv_sem=recv_sem.at[kind, k],
            device_id={"context": lax.rem(me + k + 1, n)}, device_id_type=MESH)

    def k_send(k):
        return transfer(0, k, kall.at[mine], kall.at[mine])

    def v_send(k):
        return transfer(1, k, vall.at[mine], vall.at[mine])

    def g_send(kind, k):
        return transfer(2 + kind, k, send_buf.at[kind, k], recv_buf.at[kind, k])

    loop(n - 1, lambda k: k_send(k).start())
    loop(n - 1, lambda k: v_send(k).start())

    row_copy.wait()
    keys = layout_v[...].astype(F32)
    bias_t[...] = jnp.where((keys >= start) & (keys <= token), 0.0, MASKED).T.astype(BF16)
    q_copy.wait()

    def make_q(at):
        here = span(at, chunk)
        cosines, sines = spread(cos_ref, at, chunk, heads), spread(sin_ref, at, chunk, heads)
        qe[here, :hd] = rotate(q_in[here, :].astype(F32), cosines, sines).astype(BF16)
        row = lax.broadcasted_iota(jnp.int32, (chunk, hd), 0) // heads + at * tokens
        col = lax.broadcasted_iota(jnp.int32, (chunk, hd), 1)
        qe[here, hd:] = (row == col).astype(F32).astype(BF16)

    loop(steps, make_q)
    g_copy.wait()
    loop(n - 1, lambda k: k_send(k).wait_recv())
    k_t[...] = kall[...].astype(F32).T.astype(BF16)

    def make_probs(at):
        here = span(at, chunk)
        scores = dot(jnp.concatenate([kall[...], bias_t[...]], axis=1), qe[here, :], 1)
        largest = jnp.max(scores, axis=0, keepdims=True)
        weights = jnp.exp2((scores - largest) * (scale * math.log2(math.e)))
        total = jnp.sum(weights, axis=0, keepdims=True)
        p_t[:, here] = (weights * (1.0 / total)).astype(BF16)

    loop(steps, make_probs)

    def v_grads(k):
        send_buf[0, k] = dot(p_t[span(lax.rem(me + k + 1, n), rows), :], g_in[...]).astype(BF16)
        g_send(0, k).start()

    loop(n - 1, v_grads)
    own_dv[...] = dot(p_t[mine, :], g_in[...])
    loop(n - 1, lambda k: v_send(k).wait_recv())

    def make_ds(at):
        here = span(at, chunk)
        dprobs = dot(vall[...], g_in[here, :], 1)
        p = p_t[:, here].astype(F32)
        delta = jnp.sum(p * dprobs, axis=0, keepdims=True)
        probs[:, here] = (p * (dprobs - delta) * scale).astype(BF16)

    loop(steps, make_ds)

    def k_grads(k):
        send_buf[1, k] = dot(probs[span(lax.rem(me + k + 1, n), rows), :], qe[:, :hd]).astype(BF16)
        g_send(1, k).start()

    loop(n - 1, k_grads)
    own_dk = dot(probs[mine, :], qe[:, :hd])
    v_t[...] = vall[...].astype(F32).T.astype(BF16)

    def make_o(at):
        here = span(at, chunk)
        o_ref[here, :] = dot(v_t[...], p_t[:, here]).T.astype(BF16)

    loop(steps, make_o)

    def collect(kind, own):
        loop(n - 1, lambda k: g_send(kind, k).wait_recv())
        return own + jnp.sum(recv_buf[kind].astype(F32), axis=0)

    dv_ref[...] = collect(0, own_dv[...])
    dk_ref[...] = rotate(collect(1, own_dk), cos_ref[...], -sin_ref[...])

    def finish(k):
        k_send(k).wait_send()
        v_send(k).wait_send()
        g_send(0, k).wait_send()
        g_send(1, k).wait_send()

    loop(n - 1, finish)


def last_kernel(heads, chunk, parts, o_ref, probs, k_t, cos_ref, sin_ref, dk_ref, dv_ref,
                o_h, dq_h, dk_h, dv_h, dq_buf, sem):
    flat = dq_buf.shape[0]
    copies = [pltpu.make_async_copy(src, dst, sem.at[at])
              for at, (src, dst) in enumerate(((o_ref, o_h), (dk_ref, dk_h), (dv_ref, dv_h)))]
    for copy in copies:
        copy.start()

    def make_dq(at):
        here = span(at, chunk)
        grad = dot(k_t[...], probs[:, here]).T
        cosines, sines = spread(cos_ref, at, chunk, heads), spread(sin_ref, at, chunk, heads)
        dq_buf[here, :] = rotate(grad, cosines, -sines).astype(BF16)

    steps = flat // chunk // parts
    for part in range(parts):
        loop(steps, lambda at, part=part: make_dq(at + part * steps))
        where = span(part, flat // parts)
        copy = pltpu.make_async_copy(dq_buf.at[where], dq_h.at[where], sem.at[3 + part])
        copy.start()
        copies.append(copy)
    for copy in copies:
        copy.wait()


def body(n, queries, key_heads, value_heads, out_grad, layout, documents):
    rows, heads, hd = queries.shape
    seq = layout.shape[0]
    flat = rows * heads
    small = seq <= 1024
    chunk = 256 if small else 128
    parts = 4
    hbm = pl.BlockSpec(memory_space=pltpu.HBM)
    vmem = pl.BlockSpec(memory_space=pltpu.VMEM)
    carried = pl.pallas_call(
        functools.partial(main_kernel, n, heads, chunk),
        out_shape=(
            jax.ShapeDtypeStruct((flat, hd), BF16),
            jax.ShapeDtypeStruct((seq, flat), BF16),
            jax.ShapeDtypeStruct((hd, seq), BF16),
            jax.ShapeDtypeStruct((rows, hd), F32),
            jax.ShapeDtypeStruct((rows, hd), F32),
            jax.ShapeDtypeStruct((rows, hd), F32),
            jax.ShapeDtypeStruct((rows, hd), F32),
        ),
        in_specs=[hbm] * 7,
        out_specs=(vmem,) * 7,
        scratch_shapes=[
            pltpu.SMEM((seq,), jnp.int32),
            pltpu.VMEM((1, seq), jnp.int32),
            pltpu.VMEM((1, seq), jnp.int32),
            pltpu.VMEM((rows, hd), BF16),
            pltpu.VMEM((flat, hd), BF16),
            pltpu.VMEM((flat, hd), BF16),
            pltpu.VMEM((flat, 2 * hd), BF16),
            pltpu.VMEM((seq, hd), BF16),
            pltpu.VMEM((seq, hd), BF16),
            pltpu.VMEM((hd, seq), BF16),
            pltpu.VMEM((seq, flat), BF16),
            pltpu.VMEM((seq, rows), BF16),
            pltpu.VMEM((2, n - 1, rows, hd), BF16),
            pltpu.VMEM((2, n - 1, rows, hd), BF16),
            pltpu.VMEM((rows, hd), F32),
            pltpu.SemaphoreType.DMA((7,)),
            pltpu.SemaphoreType.DMA((4, n - 1)),
            pltpu.SemaphoreType.DMA((4, n - 1)),
        ],
        compiler_params=pltpu.CompilerParams(
            collective_id=0, has_side_effects=True, vmem_limit_bytes=(32 if small else 50) * 1024 * 1024),
    )(*[pltpu.with_memory_space_constraint(operand, pltpu.HBM) for operand in (
        layout, layout.reshape(1, seq), documents.reshape(1, seq),
        queries.reshape(flat, hd), key_heads.reshape(rows, hd), value_heads.reshape(rows, hd),
        out_grad.reshape(flat, hd),
    )])
    out, dq, dk, dv = pl.pallas_call(
        functools.partial(last_kernel, heads, chunk, parts),
        out_shape=(
            jax.ShapeDtypeStruct((flat, hd), BF16),
            jax.ShapeDtypeStruct((flat, hd), BF16),
            jax.ShapeDtypeStruct((rows, hd), F32),
            jax.ShapeDtypeStruct((rows, hd), F32),
        ),
        in_specs=[vmem] * 7,
        out_specs=(hbm,) * 4,
        scratch_shapes=[pltpu.VMEM((flat, hd), BF16), pltpu.SemaphoreType.DMA((3 + parts,))],
        compiler_params=pltpu.CompilerParams(vmem_limit_bytes=(16 if small else 40) * 1024 * 1024),
    )(*carried)
    return (out.reshape(rows, heads, hd), dq.reshape(rows, heads, hd), dk, dv)


def solution(mesh):
    return jax.shard_map(
        functools.partial(body, mesh.shape["context"]),
        mesh=mesh,
        in_specs=(
            P(("dp", "context"), "tensor", None),
            P(("dp", "context"), "tensor", None),
            P(("dp", "context"), "tensor", None),
            P(("dp", "context"), "tensor", None),
            P("dp"),
            P("dp"),
        ),
        out_specs=(
            P(("dp", "context"), "tensor", None),
            P(("dp", "context"), "tensor", None),
            P(("dp", "context"), "tensor"),
            P(("dp", "context"), "tensor"),
        ),
        check_vma=False,
    )
```

time: 26.6 us -> 17.5 us (0.66)
  local copies, waits for them, and re-layouts: 6.08 us -> 0 us
  Pallas kernels: 19.5 us -> 16.7 us
    unnamed x14 -> x0, local copies, waits for them, and re-layouts: 6.08 us -> none
    pallas_call x1 -> x2, Pallas kernels: 19.5 us -> 16.7 us  [the longest x1 15.1 us: body(): pl.pallas_call(functools.partial(main_kernel, n, heads, chunk), out_shape...]
where the time goes in v2:
time: 17.5 us; the launch traced here: 17.3 us
  Pallas kernels  16.7 us (95%)
  between operations  0.64 us (4%)
    pallas_call x1, Pallas kernels, body(): pl.pallas_call(functools.partial(main_kernel, n, heads, chunk), out_shape...  15.1 us
    pallas_call x1, Pallas kernels, body(): pl.pallas_call(functools.partial(last_kernel, heads, chunk, parts), out_s...  1.57 us

profile of v2, /device:TPU:0, one launch (start us, length us, event | category | flops | bytes accessed | tf_op | source)
XLA Modules:
  0.0 17.3 jit_solution(9882915898224982180)
XLA Ops:
  0.6 15.1 %shard_map.93 = (bf16[2048,128]{1,0:T(8,128)(2,1)S(1)}, bf16[512,2048]{1,0:T(8,128)(2,1)S(1)}, bf16[128,512]{1,0:T(8,128)(2,1)S(1)}, f32[128,128]{1,0:T(8,128)S(...) custom-call(s32[512]{0:T(512)} %layout_h.1, s32[1,512]{1,0:T(1,128)} %bitcast.12, ...), custom_call_target="tpu_custom_call" | custom-call | tf_op jit(solution)/shard_map/pallas_call | solution.py:224
  15.7 1.6 %shard_map.94 = (bf16[2048,128]{1,0:T(8,128)(2,1)}, bf16[2048,128]{1,0:T(8,128)(2,1)}, f32[128,128]{1,0:T(8,128)}, f32[128,128]{1,0:T(8,128)}) custom-call(bf16[2048,128]{1,0:T(8,128)(2,1)S(1)} %get-tuple-element.15.o_ref, bf16[512,2048]{1,0:T(8,128)(2,1)S(1)} %get-tuple-element.16.probs, bf16[128,512]{1,0:T(8,128)(2,1)S(1)} %get-tuple-element.17.k_t, ...), custom_call_target="tpu_custom_call" | custom-call | tf_op jit(solution)/shard_map/pallas_call | solution.py:264

commit v3 on v2

--- a/solution.py
+++ b/solution.py
@@ -43,8 +43,8 @@
 
 
 def main_kernel(n, heads, chunk, layout_h, layout_row_h, docs_h, q_h, k_h, v_h, g_h,
-                o_ref, probs, k_t, cos_ref, sin_ref, dk_ref, dv_ref,
-                layout_s, layout_v, docs_v, k_in, q_in, g_in, qe, kall, vall, v_t, p_t, bias_t,
+                o_ref, dq_ref, dk_ref, dv_ref,
+                probs, k_t, cos_ref, sin_ref, w_near, stats, layout_s, layout_v, docs_v, k_in, q_in, g_in, qe, kall, vall, v_t, p_t, bias_t,
                 send_buf, recv_buf, own_dv, local_sem, send_sem, recv_sem):
     me = lax.axis_index("context")
     rows, hd = k_in.shape
@@ -54,9 +54,15 @@
     steps = flat // chunk
     scale = 1.0 / math.sqrt(hd)
 
+    factor = scale * math.log2(math.e)
+
+    def peer(k):
+        pair = lax.rem(me // 2 + (k + 1) // 2, n // 2)
+        return pair * 2 + lax.rem(me + k + 1, 2)
+
     barrier = pltpu.get_barrier_semaphore()
-    for k in range(1, n):
-        pl.semaphore_signal(barrier, inc=1, device_id={"context": lax.rem(me + k, n)}, device_id_type=MESH)
+    for k in range(n - 1):
+        pl.semaphore_signal(barrier, inc=1, device_id={"context": peer(k)}, device_id_type=MESH)
 
     mine = span(me, rows)
     layout_copy = pltpu.make_async_copy(layout_h, layout_s, local_sem.at[0])
@@ -98,7 +104,7 @@
         return pltpu.make_async_remote_copy(
             src_ref=source, dst_ref=target,
             send_sem=send_sem.at[kind, k], recv_sem=recv_sem.at[kind, k],
-            device_id={"context": lax.rem(me + k + 1, n)}, device_id_type=MESH)
+            device_id={"context": peer(k)}, device_id_type=MESH)
 
     def k_send(k):
         return transfer(0, k, kall.at[mine], kall.at[mine])
@@ -109,8 +115,7 @@
     def g_send(kind, k):
         return transfer(2 + kind, k, send_buf.at[kind, k], recv_buf.at[kind, k])
 
-    loop(n - 1, lambda k: k_send(k).start())
-    loop(n - 1, lambda k: v_send(k).start())
+    loop(n - 1, lambda k: k_send(n - 2 - k).start())
 
     row_copy.wait()
     keys = layout_v[...].astype(F32)
@@ -126,26 +131,56 @@
         qe[here, hd:] = (row == col).astype(F32).astype(BF16)
 
     loop(steps, make_q)
-    g_copy.wait()
-    loop(n - 1, lambda k: k_send(k).wait_recv())
-    k_t[...] = kall[...].astype(F32).T.astype(BF16)
 
     def make_probs(at):
         here = span(at, chunk)
         scores = dot(jnp.concatenate([kall[...], bias_t[...]], axis=1), qe[here, :], 1)
         largest = jnp.max(scores, axis=0, keepdims=True)
-        weights = jnp.exp2((scores - largest) * (scale * math.log2(math.e)))
+        weights = jnp.exp2((scores - largest) * factor)
         total = jnp.sum(weights, axis=0, keepdims=True)
         p_t[:, here] = (weights * (1.0 / total)).astype(BF16)
 
-    loop(steps, make_probs)
+    near = span(me // 2, 2 * rows)
+    far = span(1 - me // 2, 2 * rows)
+
+    def make_near(at):
+        here = span(at, chunk)
+        scores = dot(jnp.concatenate([kall[near, :], bias_t[near, :]], axis=1), qe[here, :], 1)
+        largest = jnp.max(scores, axis=0, keepdims=True)
+        weights = jnp.exp2((scores - largest) * factor)
+        w_near[:, here] = weights
+        stats[0:1, here] = largest
+        stats[1:2, here] = jnp.sum(weights, axis=0, keepdims=True)
+
+    def make_far(at):
+        here = span(at, chunk)
+        scores = dot(jnp.concatenate([kall[far, :], bias_t[far, :]], axis=1), qe[here, :], 1)
+        near_largest = stats[0:1, here]
+        largest = jnp.maximum(near_largest, jnp.max(scores, axis=0, keepdims=True))
+        weights = jnp.exp2((scores - largest) * factor)
+        shrink = jnp.exp2((near_largest - largest) * factor)
+        inverse = 1.0 / (stats[1:2, here] * shrink + jnp.sum(weights, axis=0, keepdims=True))
+        p_t[far, here] = (weights * inverse).astype(BF16)
+        p_t[near, here] = (w_near[:, here] * (shrink * inverse)).astype(BF16)
+
+    if n == 4:
+        k_send(0).wait_recv()
+        loop(steps, make_near)
+        k_send(1).wait_recv()
+        k_send(2).wait_recv()
+        loop(n - 1, lambda k: v_send(n - 2 - k).start())
+        loop(steps, make_far)
+    else:
+        loop(n - 1, lambda k: k_send(k).wait_recv())
+        loop(n - 1, lambda k: v_send(k).start())
+        loop(steps, make_probs)
+    g_copy.wait()
 
     def v_grads(k):
-        send_buf[0, k] = dot(p_t[span(lax.rem(me + k + 1, n), rows), :], g_in[...]).astype(BF16)
+        send_buf[0, k] = dot(p_t[span(peer(k), rows), :], g_in[...]).astype(BF16)
         g_send(0, k).start()
 
-    loop(n - 1, v_grads)
-    own_dv[...] = dot(p_t[mine, :], g_in[...])
+    loop(n - 1, lambda k: v_grads(n - 2 - k))
     loop(n - 1, lambda k: v_send(k).wait_recv())
 
     def make_ds(at):
@@ -153,23 +188,32 @@
         dprobs = dot(vall[...], g_in[here, :], 1)
         p = p_t[:, here].astype(F32)
         delta = jnp.sum(p * dprobs, axis=0, keepdims=True)
-        probs[:, here] = (p * (dprobs - delta) * scale).astype(BF16)
+        probs[:, here] = (p * (dprobs - delta)).astype(BF16)
 
     loop(steps, make_ds)
 
     def k_grads(k):
-        send_buf[1, k] = dot(probs[span(lax.rem(me + k + 1, n), rows), :], qe[:, :hd]).astype(BF16)
+        send_buf[1, k] = (dot(probs[span(peer(k), rows), :], qe[:, :hd]) * scale).astype(BF16)
         g_send(1, k).start()
 
-    loop(n - 1, k_grads)
-    own_dk = dot(probs[mine, :], qe[:, :hd])
+    loop(n - 1, lambda k: k_grads(n - 2 - k))
+    own_dk = dot(probs[mine, :], qe[:, :hd]) * scale
+    own_dv[...] = dot(p_t[mine, :], g_in[...])
+    k_t[...] = kall[...].astype(F32).T.astype(BF16)
     v_t[...] = vall[...].astype(F32).T.astype(BF16)
 
     def make_o(at):
         here = span(at, chunk)
         o_ref[here, :] = dot(v_t[...], p_t[:, here]).T.astype(BF16)
 
+    def make_dq(at):
+        here = span(at, chunk)
+        grad = dot(k_t[...], probs[:, here]).T * scale
+        cosines, sines = spread(cos_ref, at, chunk, heads), spread(sin_ref, at, chunk, heads)
+        dq_ref[here, :] = rotate(grad, cosines, -sines).astype(BF16)
+
     loop(steps, make_o)
+    loop(steps, make_dq)
 
     def collect(kind, own):
         loop(n - 1, lambda k: g_send(kind, k).wait_recv())
@@ -187,27 +231,12 @@
     loop(n - 1, finish)
 
 
-def last_kernel(heads, chunk, parts, o_ref, probs, k_t, cos_ref, sin_ref, dk_ref, dv_ref,
-                o_h, dq_h, dk_h, dv_h, dq_buf, sem):
-    flat = dq_buf.shape[0]
-    copies = [pltpu.make_async_copy(src, dst, sem.at[at])
-              for at, (src, dst) in enumerate(((o_ref, o_h), (dk_ref, dk_h), (dv_ref, dv_h)))]
+def last_kernel(*refs):
+    count = len(refs) // 2
+    sem = refs[-1]
+    copies = [pltpu.make_async_copy(refs[at], refs[count + at], sem.at[at]) for at in range(count)]
     for copy in copies:
         copy.start()
-
-    def make_dq(at):
-        here = span(at, chunk)
-        grad = dot(k_t[...], probs[:, here]).T
-        cosines, sines = spread(cos_ref, at, chunk, heads), spread(sin_ref, at, chunk, heads)
-        dq_buf[here, :] = rotate(grad, cosines, -sines).astype(BF16)
-
-    steps = flat // chunk // parts
-    for part in range(parts):
-        loop(steps, lambda at, part=part: make_dq(at + part * steps))
-        where = span(part, flat // parts)
-        copy = pltpu.make_async_copy(dq_buf.at[where], dq_h.at[where], sem.at[3 + part])
-        copy.start()
-        copies.append(copy)
     for copy in copies:
         copy.wait()
 
@@ -218,23 +247,26 @@
     flat = rows * heads
     small = seq <= 1024
     chunk = 256 if small else 128
-    parts = 4
     hbm = pl.BlockSpec(memory_space=pltpu.HBM)
     vmem = pl.BlockSpec(memory_space=pltpu.VMEM)
+    shapes = (
+        jax.ShapeDtypeStruct((flat, hd), BF16),
+        jax.ShapeDtypeStruct((flat, hd), BF16),
+        jax.ShapeDtypeStruct((rows, hd), F32),
+        jax.ShapeDtypeStruct((rows, hd), F32),
+    )
     carried = pl.pallas_call(
         functools.partial(main_kernel, n, heads, chunk),
-        out_shape=(
-            jax.ShapeDtypeStruct((flat, hd), BF16),
-            jax.ShapeDtypeStruct((seq, flat), BF16),
-            jax.ShapeDtypeStruct((hd, seq), BF16),
-            jax.ShapeDtypeStruct((rows, hd), F32),
-            jax.ShapeDtypeStruct((rows, hd), F32),
-            jax.ShapeDtypeStruct((rows, hd), F32),
-            jax.ShapeDtypeStruct((rows, hd), F32),
-        ),
+        out_shape=shapes,
         in_specs=[hbm] * 7,
-        out_specs=(vmem,) * 7,
+        out_specs=(vmem,) * 4,
         scratch_shapes=[
+            pltpu.VMEM((seq, flat), BF16),
+            pltpu.VMEM((hd, seq), BF16),
+            pltpu.VMEM((rows, hd), F32),
+            pltpu.VMEM((rows, hd), F32),
+            pltpu.VMEM((2 * rows if n == 4 else 8, flat), F32),
+            pltpu.VMEM((8, flat), F32),
             pltpu.SMEM((seq,), jnp.int32),
             pltpu.VMEM((1, seq), jnp.int32),
             pltpu.VMEM((1, seq), jnp.int32),
@@ -255,24 +287,19 @@
             pltpu.SemaphoreType.DMA((4, n - 1)),
         ],
         compiler_params=pltpu.CompilerParams(
-            collective_id=0, has_side_effects=True, vmem_limit_bytes=(32 if small else 50) * 1024 * 1024),
+            collective_id=0, has_side_effects=True, vmem_limit_bytes=(40 if small else 58) * 1024 * 1024),
     )(*[pltpu.with_memory_space_constraint(operand, pltpu.HBM) for operand in (
         layout, layout.reshape(1, seq), documents.reshape(1, seq),
         queries.reshape(flat, hd), key_heads.reshape(rows, hd), value_heads.reshape(rows, hd),
         out_grad.reshape(flat, hd),
     )])
     out, dq, dk, dv = pl.pallas_call(
-        functools.partial(last_kernel, heads, chunk, parts),
-        out_shape=(
-            jax.ShapeDtypeStruct((flat, hd), BF16),
-            jax.ShapeDtypeStruct((flat, hd), BF16),
-            jax.ShapeDtypeStruct((rows, hd), F32),
-            jax.ShapeDtypeStruct((rows, hd), F32),
-        ),
-        in_specs=[vmem] * 7,
+        last_kernel,
+        out_shape=shapes,
+        in_specs=[vmem] * 4,
         out_specs=(hbm,) * 4,
-        scratch_shapes=[pltpu.VMEM((flat, hd), BF16), pltpu.SemaphoreType.DMA((3 + parts,))],
-        compiler_params=pltpu.CompilerParams(vmem_limit_bytes=(16 if small else 40) * 1024 * 1024),
+        scratch_shapes=[pltpu.SemaphoreType.DMA((4,))],
+        compiler_params=pltpu.CompilerParams(vmem_limit_bytes=8 * 1024 * 1024),
     )(*carried)
     return (out.reshape(rows, heads, hd), dq.reshape(rows, heads, hd), dk, dv)
 

time: 17.5 us -> 17.4 us (level)
    pallas_call x1, Pallas kernels: 1.57 us -> 1.03 us  [body(): pl.pallas_call(last_kernel, out_shape=shapes, in_specs=[vmem] * 4, out_sp...]
    pallas_call x1, Pallas kernels: 15.1 us -> 15.5 us  [body(): pl.pallas_call(functools.partial(main_kernel, n, heads, chunk), out_shape...]
where the time goes in v3:
time: 17.4 us; the launch traced here: 17.2 us
  Pallas kernels  16.6 us (95%)
  between operations  0.64 us (4%)
    pallas_call x1, Pallas kernels, body(): pl.pallas_call(functools.partial(main_kernel, n, heads, chunk), out_shape...  15.5 us
    pallas_call x1, Pallas kernels, body(): pl.pallas_call(last_kernel, out_shape=shapes, in_specs=[vmem] * 4, out_sp...  1.03 us

profile of v3, /device:TPU:0, one launch (start us, length us, event | category | flops | bytes accessed | tf_op | source)
XLA Modules:
  0.0 17.2 jit_solution(9302957978345881163)
XLA Ops:
  0.6 15.5 %shard_map.93 = (bf16[2048,128]{1,0:T(8,128)(2,1)S(1)}, bf16[2048,128]{1,0:T(8,128)(2,1)S(1)}, f32[128,128]{1,0:T(8,128)S(1)}, f32[128,128]{1,0:T(8,128)S(1)}) custom-call(s32[512]{0:T(512)} %layout_h.1, s32[1,512]{1,0:T(1,128)} %bitcast.12, s32[1,512]{1,0:T(1,128)} %bitcast.13, bf16[2048,128]{1,0:T(8,128)(2,1)} %bitcast.8, bf16[128,128]{1,0:T(8,128)(2,1)} %bitcast.10, ...), custom_call_target="tpu_custom_call" | custom-call | tf_op jit(solution)/shard_map/pallas_call | solution.py:258
  16.2 1.0 %shard_map.94 = (bf16[2048,128]{1,0:T(8,128)(2,1)}, bf16[2048,128]{1,0:T(8,128)(2,1)}, f32[128,128]{1,0:T(8,128)}, f32[128,128]{1,0:T(8,128)}) custom-call(bf16[2048,128]{1,0:T(8,128)(2,1)S(1)} %get-tuple-element.12.refs_0_, bf16[2048,128]{1,0:T(8,128)(2,1)S(1)} %get-tuple-element.13.refs_1_, f32[128,128]{1,0:T(8,128)S(1)} %get-tuple-element.14.refs_2_, ...), custom_call_target="tpu_custom_call" | custom-call | tf_op jit(solution)/shard_map/pallas_call | solution.py:296

commit v4 on v3

--- a/solution.py
+++ b/solution.py
@@ -116,6 +116,8 @@
         return transfer(2 + kind, k, send_buf.at[kind, k], recv_buf.at[kind, k])
 
     loop(n - 1, lambda k: k_send(n - 2 - k).start())
+    if n == 4:
+        loop(n - 1, lambda k: v_send(n - 2 - k).start())
 
     row_copy.wait()
     keys = layout_v[...].astype(F32)
@@ -168,7 +170,6 @@
         loop(steps, make_near)
         k_send(1).wait_recv()
         k_send(2).wait_recv()
-        loop(n - 1, lambda k: v_send(n - 2 - k).start())
         loop(steps, make_far)
     else:
         loop(n - 1, lambda k: k_send(k).wait_recv())

time: 17.4 us -> 16.3 us (0.937)
  Pallas kernels: 16.6 us -> 15.5 us
    pallas_call x1, Pallas kernels: 15.5 us -> 14.5 us  [body(): pl.pallas_call(functools.partial(main_kernel, n, heads, chunk), out_shape...]
where the time goes in v4:
time: 16.3 us; the launch traced here: 16.2 us
  Pallas kernels  15.5 us (95%)
  between operations  0.64 us (4%)
    pallas_call x1, Pallas kernels, body(): pl.pallas_call(functools.partial(main_kernel, n, heads, chunk), out_shape...  14.5 us
    pallas_call x1, Pallas kernels, body(): pl.pallas_call(last_kernel, out_shape=shapes, in_specs=[vmem] * 4, out_sp...  1.03 us

profile of v4, /device:TPU:0, one launch (start us, length us, event | category | flops | bytes accessed | tf_op | source)
XLA Modules:
  0.0 16.2 jit_solution(13920390857131478742)
XLA Ops:
  0.6 14.5 %shard_map.93 = (bf16[2048,128]{1,0:T(8,128)(2,1)S(1)}, bf16[2048,128]{1,0:T(8,128)(2,1)S(1)}, f32[128,128]{1,0:T(8,128)S(1)}, f32[128,128]{1,0:T(8,128)S(1)}) custom-call(s32[512]{0:T(512)} %layout_h.1, s32[1,512]{1,0:T(1,128)} %bitcast.12, s32[1,512]{1,0:T(1,128)} %bitcast.13, bf16[2048,128]{1,0:T(8,128)(2,1)} %bitcast.8, bf16[128,128]{1,0:T(8,128)(2,1)} %bitcast.10, ...), custom_call_target="tpu_custom_call" | custom-call | tf_op jit(solution)/shard_map/pallas_call | solution.py:259
  15.1 1.0 %shard_map.94 = (bf16[2048,128]{1,0:T(8,128)(2,1)}, bf16[2048,128]{1,0:T(8,128)(2,1)}, f32[128,128]{1,0:T(8,128)}, f32[128,128]{1,0:T(8,128)}) custom-call(bf16[2048,128]{1,0:T(8,128)(2,1)S(1)} %get-tuple-element.12.refs_0_, bf16[2048,128]{1,0:T(8,128)(2,1)S(1)} %get-tuple-element.13.refs_1_, f32[128,128]{1,0:T(8,128)S(1)} %get-tuple-element.14.refs_2_, ...), custom_call_target="tpu_custom_call" | custom-call | tf_op jit(solution)/shard_map/pallas_call | solution.py:297
